TPU v7x, 32 devices: a whole 2x2x4 slice. The times are simulated.
32 devices in a mesh: tm: 8 (over y, x, core), space: 4 (over z).
Axes of the slice: x: 2, y: 2, z: 4, core: 2. Of those that a mesh axis runs over, the one named last changes fastest.
Arguments:
- steps: bfloat16 [24, 1024, 1024], P('tm', 'space'), as said below
- lengths: int32 [8], P('tm'), may hold values from 1 to 3, 16 in all
- anchor: bfloat16 [1024, 2048], P(None, 'space'), may hold values from -6 to 6
Outputs:
- panels: float32 [24, 1024, 2048], P('tm', None, 'space')
Inputs may be any that keep to these rules, and one draw needn't show every extreme that they name: `steps`: slots of a section beyond its length hold entries that no output reads.
All inputs are finite; a program needn't handle non-finite values. No bound on the sum of `lengths` on one device may be relied on, other than what follows from the above.
Results may differ from a plain program's by a relative error of at most 0.025.
Values may be sent and summed in bfloat16 or wider, within the bound.
A program may use at most 64 MiB of HBM per device.

v0:
```python
import jax
import jax.numpy as jnp
from jax import lax
from jax.sharding import PartitionSpec as P


def from_behind(block, axis, distance):
    devices = range(lax.axis_size(axis))
    route = [(i - distance, i) for i in devices if i - distance in devices]
    return lax.ppermute(block, axis, route)


def run_section(blocks, section_count, incoming, results, offset):
    capacity = blocks.shape[0]
    for slot in range(capacity - 1, -1, -1):

        def live(state, slot=slot):
            carry_in, stored = state
            value = jnp.dot(blocks[slot], carry_in, preferred_element_type=jnp.float32)
            stored = lax.dynamic_update_slice(stored, value[None], (slot, 0, offset))
            return (value.astype(jnp.bfloat16), stored)

        incoming, results = lax.cond(
            slot < section_count, live, lambda state: state, (incoming, results)
        )
    return (incoming, results)


def shards(steps, lengths, anchor):
    capacity, width = (steps.shape[0], anchor.shape[1])
    rows = anchor.shape[0]
    segments = lax.axis_size("tm")
    me = lax.axis_index("tm")
    section_count = lengths[0]
    blocks = lax.all_gather(steps, "space", axis=1, tiled=True)
    results = jnp.zeros((capacity, rows, width), jnp.float32)

    def segment(k, state):
        incoming, stored = state
        active = me == segments - 1 - k
        incoming, stored = lax.cond(
            active,
            lambda s: run_section(blocks, section_count, s[0], s[1], 0),
            lambda s: s,
            (incoming, stored),
        )
        incoming = from_behind(incoming, "tm", -1)
        return (incoming, stored)

    final, results = lax.fori_loop(0, segments, segment, (anchor, results))
    return results


def solution(mesh):
    return jax.shard_map(
        shards,
        mesh=mesh,
        in_specs=(P("tm", "space", None), P("tm"), P(None, "space")),
        out_specs=P("tm", None, "space"),
        check_vma=False,
    )
```

profile of v0, /device:TPU:1, one launch (start us, length us, event | category | flops | bytes accessed | tf_op | source)
XLA Modules:
  0.0 314.1 jit_solution(14158469819239776622)
XLA Ops:
  6.5 0.0 copy-start
  6.5 0.0 all-gather.2.cloned.1.call-start
  6.5 0.7 all-gather.2.cloned.1.call-update
  7.3 119.2 %all-gather.2.cloned.1.call-done = bf16[3,1024,1024]{2,1,0:T(8,128)(2,1)} async-done(((bf16[3,256,1024]{2,1,0:T(8,128)(2,1)}), bf16[3,1024,1024]{2,1,0:T(8,128)(2,1)}) %all-gather.2.cloned.1.call-update) | async-done | bytes 6291472 | tf_op jit(solution)/shard_map/all_gather | solution.py:35
  126.5 3.5 %broadcast_in_dim.12 = f32[3,1024,512]{2,1,0:T(8,128)} broadcast(f32[]{:T(128)} %constant.39.clone.1), dimensions={} | broadcast | bytes 6291460 | tf_op jit(solution)/shard_map/broadcast_in_dim | solution.py:36
  130.0 0.0 copy-done
  130.0 177.3 %while.15 = (s32[]{:T(128)}, bf16[1024,512]{1,0:T(8,128)(2,1)S(1)}, f32[3,1024,512]{2,1,0:T(8,128)}, s32[]{:T(128)}, s32[]{:T(128)}, /*index=5*/bf16[3,1024,1024]{2,1,0:T(8,128)(2,1)}, s32[]{:T(128)}, s32[]{:T(128)}) while((s32[]{:T(128)}, bf16[1024,512]{1,0:T(8,128)(2,1)S(1)}, f32[3,1024,512]{2,1,0:T(8,128)}, s32[]{:T(128)}, s32[]{:T(128)}, ...), condition=%wide.region_9.0_spmd, body=%wide.region_0.0_spmd.sunk | while | flops 3222798336 | bytes 44040592 | solution.py:50
  130.0 2.4 collective-permute-start
  132.4 13.7 %collective-permute-done = bf16[1024,512]{1,0:T(8,128)(2,1)S(1)} collective-permute-done((bf16[1024,512]{1,0:T(8,128)(2,1)S(1)}, bf16[1024,512]{1,0:T(8,128)(2,1)S(1)}, u32[]{:S(2)}, u32[]{:S(2)}) %collective-permute-start) | collective-permute-done | bytes 1048608 | tf_op jit(solution)/shard_map/while/body/eval_jaxpr/ppermute | solution.py:10
  146.1 0.1 copy.30
  146.2 1.9 collective-permute-start
  148.2 14.2 %collective-permute-done = bf16[1024,512]{1,0:T(8,128)(2,1)S(1)} collective-permute-done((bf16[1024,512]{1,0:T(8,128)(2,1)S(1)}, bf16[1024,512]{1,0:T(8,128)(2,1)S(1)}, u32[]{:S(2)}, u32[]{:S(2)}) %collective-permute-start) | collective-permute-done | bytes 1048608 | tf_op jit(solution)/shard_map/while/body/eval_jaxpr/ppermute | solution.py:10
  162.3 0.1 copy.30
  162.5 1.9 collective-permute-start
  164.4 14.2 %collective-permute-done = bf16[1024,512]{1,0:T(8,128)(2,1)S(1)} collective-permute-done((bf16[1024,512]{1,0:T(8,128)(2,1)S(1)}, bf16[1024,512]{1,0:T(8,128)(2,1)S(1)}, u32[]{:S(2)}, u32[]{:S(2)}) %collective-permute-start) | collective-permute-done | bytes 1048608 | tf_op jit(solution)/shard_map/while/body/eval_jaxpr/ppermute | solution.py:10
  178.6 0.1 copy.30
  178.7 1.9 collective-permute-start
  180.6 14.2 %collective-permute-done = bf16[1024,512]{1,0:T(8,128)(2,1)S(1)} collective-permute-done((bf16[1024,512]{1,0:T(8,128)(2,1)S(1)}, bf16[1024,512]{1,0:T(8,128)(2,1)S(1)}, u32[]{:S(2)}, u32[]{:S(2)}) %collective-permute-start) | collective-permute-done | bytes 1048608 | tf_op jit(solution)/shard_map/while/body/eval_jaxpr/ppermute | solution.py:10
  194.8 0.1 copy.30
  194.9 1.9 collective-permute-start
  196.9 14.2 %collective-permute-done = bf16[1024,512]{1,0:T(8,128)(2,1)S(1)} collective-permute-done((bf16[1024,512]{1,0:T(8,128)(2,1)S(1)}, bf16[1024,512]{1,0:T(8,128)(2,1)S(1)}, u32[]{:S(2)}, u32[]{:S(2)}) %collective-permute-start) | collective-permute-done | bytes 1048608 | tf_op jit(solution)/shard_map/while/body/eval_jaxpr/ppermute | solution.py:10
  211.1 0.1 copy.30
  211.2 1.9 collective-permute-start
  213.1 46.4 %collective-permute-done = bf16[1024,512]{1,0:T(8,128)(2,1)S(1)} collective-permute-done((bf16[1024,512]{1,0:T(8,128)(2,1)S(1)}, bf16[1024,512]{1,0:T(8,128)(2,1)S(1)}, u32[]{:S(2)}, u32[]{:S(2)}) %collective-permute-start) | collective-permute-done | bytes 1048608 | tf_op jit(solution)/shard_map/while/body/eval_jaxpr/ppermute | solution.py:10
  259.5 0.1 copy.30
  259.6 15.3 %conditional.5 = ((bf16[1024,512]{1,0:T(8,128)(2,1)S(1)}, f32[3,1024,512]{2,1,0:T(8,128)})) conditional(s32[]{:T(128)} %convert_element_type.29, (bf16[1024,512]{1,0:T(8,128)(2,1)S(1)}, f32[3,1024,512]{2,1,0:T(8,128)}) %tuple.58, (s32[]{:T(128)}, bf16[1024,512]{1,0:T(8,128)(2,1)S(1)}, f32[3,1024,512]{2,1,0:T(8,128)}, ...), branch_computations={%region_1.0_spmd, %region_2.0_spmd} | conditional | flops 3222798336 | bytes 37748936 | solution.py:41
  260.2 4.4 %conditional = ((bf16[1024,512]{1,0:T(8,128)(2,1)S(1)}, f32[3,1024,512]{2,1,0:T(8,128)})) conditional(s32[]{:T(128)} %convert_element_type.23, (bf16[1024,512]{1,0:T(8,128)(2,1)S(1)}, f32[3,1024,512]{2,1,0:T(8,128)}) %tuple.36, (bf16[3,1024,1024]{2,1,0:T(8,128)(2,1)}, bf16[1024,512]{1,0:T(8,128)(2,1)S(1)}, f32[3,1024,512]{2,1,0:T(8,128)}) %tuple.37), branch_computations={%region_3.0_spmd, %region_4.0_spmd} | conditional | flops 1074266112 | bytes 12582936 | solution.py:23
  260.3 0.1 copy.32
  260.3 2.8 fusion.9
  263.2 1.5 bitcast_dynamic-update-slice_fusion
  265.3 4.4 %conditional.1 = ((bf16[1024,512]{1,0:T(8,128)(2,1)S(1)}, f32[3,1024,512]{2,1,0:T(8,128)})) conditional(s32[]{:T(128)} %convert_element_type.22, (bf16[1024,512]{1,0:T(8,128)(2,1)S(1)}, f32[3,1024,512]{2,1,0:T(8,128)}) %get-tuple-element.277, (bf16[3,1024,1024]{2,1,0:T(8,128)(2,1)}, bf16[1024,512]{1,0:T(8,128)(2,1)S(1)}, ...), branch_computations={%region_5.0_spmd, %region_6.0_spmd} | conditional | flops 1074266112 | bytes 12582936 | solution.py:23
  265.3 0.1 copy.33
  265.4 2.8 fusion.10
  268.3 1.5 bitcast_dynamic-update-slice_fusion.1
  270.4 4.4 %conditional.2 = ((bf16[1024,512]{1,0:T(8,128)(2,1)S(1)}, f32[3,1024,512]{2,1,0:T(8,128)})) conditional(s32[]{:T(128)} %convert_element_type.21, (bf16[1024,512]{1,0:T(8,128)(2,1)S(1)}, f32[3,1024,512]{2,1,0:T(8,128)}) %get-tuple-element.278, (bf16[3,1024,1024]{2,1,0:T(8,128)(2,1)}, bf16[1024,512]{1,0:T(8,128)(2,1)S(1)}, ...), branch_computations={%region_7.0_spmd, %region_8.0_spmd} | conditional | flops 1074266112 | bytes 12582936 | solution.py:23
  270.4 0.1 copy.34
  270.5 2.8 fusion.11
  273.4 1.5 bitcast_dynamic-update-slice_fusion.2
  274.8 1.9 collective-permute-start
  276.8 14.2 %collective-permute-done = bf16[1024,512]{1,0:T(8,128)(2,1)S(1)} collective-permute-done((bf16[1024,512]{1,0:T(8,128)(2,1)S(1)}, bf16[1024,512]{1,0:T(8,128)(2,1)S(1)}, u32[]{:S(2)}, u32[]{:S(2)}) %collective-permute-start) | collective-permute-done | bytes 1048608 | tf_op jit(solution)/shard_map/while/body/eval_jaxpr/ppermute | solution.py:10
  291.0 0.1 copy.30
  291.1 1.9 collective-permute-start
  293.0 14.2 %collective-permute-done = bf16[1024,512]{1,0:T(8,128)(2,1)S(1)} collective-permute-done((bf16[1024,512]{1,0:T(8,128)(2,1)S(1)}, bf16[1024,512]{1,0:T(8,128)(2,1)S(1)}, u32[]{:S(2)}, u32[]{:S(2)}) %collective-permute-start) | collective-permute-done | bytes 1048608 | tf_op jit(solution)/shard_map/while/body/eval_jaxpr/ppermute | solution.py:10
  307.2 0.1 copy.30
  (7 shorter events, 0.1 us)
Async XLA Ops:
  6.5 123.5 %copy-start = (bf16[1024,512]{1,0:T(8,128)(2,1)S(1)}, bf16[1024,512]{1,0:T(8,128)(2,1)}, u32[]{:S(2)}) copy-start(bf16[1024,512]{1,0:T(8,128)(2,1)} %param.15) | copy-start | bytes 3145732
  6.5 120.0 %all-gather.2.cloned.1.call-start = ((), (), s32[]{:S(2)}) async-start(), calls=%async_computation | async-start | bytes 7864320 | tf_op jit(solution)/shard_map/all_gather | solution.py:35
  130.0 16.1 %collective-permute-start = (bf16[1024,512]{1,0:T(8,128)(2,1)S(1)}, bf16[1024,512]{1,0:T(8,128)(2,1)S(1)}, u32[]{:S(2)}, u32[]{:S(2)}) collective-permute-start(bf16[1024,512]{1,0:T(8,128)(2,1)S(1)} %get-tuple-element.235), channel_id=1, source_target_pairs={{4,0},{8,4},{12,8},{16,12},{20,16},{24,20},{28,24},{5,1},{9,5},{13... | collective-permute-start | bytes 3145736 | tf_op jit(solution)/shard_map/while/body/eval_jaxpr/ppermute | solution.py:10
  146.2 16.1 %collective-permute-start = (bf16[1024,512]{1,0:T(8,128)(2,1)S(1)}, bf16[1024,512]{1,0:T(8,128)(2,1)S(1)}, u32[]{:S(2)}, u32[]{:S(2)}) collective-permute-start(bf16[1024,512]{1,0:T(8,128)(2,1)S(1)} %get-tuple-element.235), channel_id=1, source_target_pairs={{4,0},{8,4},{12,8},{16,12},{20,16},{24,20},{28,24},{5,1},{9,5},{13... | collective-permute-start | bytes 3145736 | tf_op jit(solution)/shard_map/while/body/eval_jaxpr/ppermute | solution.py:10
  162.5 16.1 %collective-permute-start = (bf16[1024,512]{1,0:T(8,128)(2,1)S(1)}, bf16[1024,512]{1,0:T(8,128)(2,1)S(1)}, u32[]{:S(2)}, u32[]{:S(2)}) collective-permute-start(bf16[1024,512]{1,0:T(8,128)(2,1)S(1)} %get-tuple-element.235), channel_id=1, source_target_pairs={{4,0},{8,4},{12,8},{16,12},{20,16},{24,20},{28,24},{5,1},{9,5},{13... | collective-permute-start | bytes 3145736 | tf_op jit(solution)/shard_map/while/body/eval_jaxpr/ppermute | solution.py:10
  178.7 16.1 %collective-permute-start = (bf16[1024,512]{1,0:T(8,128)(2,1)S(1)}, bf16[1024,512]{1,0:T(8,128)(2,1)S(1)}, u32[]{:S(2)}, u32[]{:S(2)}) collective-permute-start(bf16[1024,512]{1,0:T(8,128)(2,1)S(1)} %get-tuple-element.235), channel_id=1, source_target_pairs={{4,0},{8,4},{12,8},{16,12},{20,16},{24,20},{28,24},{5,1},{9,5},{13... | collective-permute-start | bytes 3145736 | tf_op jit(solution)/shard_map/while/body/eval_jaxpr/ppermute | solution.py:10
  194.9 16.1 %collective-permute-start = (bf16[1024,512]{1,0:T(8,128)(2,1)S(1)}, bf16[1024,512]{1,0:T(8,128)(2,1)S(1)}, u32[]{:S(2)}, u32[]{:S(2)}) collective-permute-start(bf16[1024,512]{1,0:T(8,128)(2,1)S(1)} %get-tuple-element.235), channel_id=1, source_target_pairs={{4,0},{8,4},{12,8},{16,12},{20,16},{24,20},{28,24},{5,1},{9,5},{13... | collective-permute-start | bytes 3145736 | tf_op jit(solution)/shard_map/while/body/eval_jaxpr/ppermute | solution.py:10
  211.2 48.3 %collective-permute-start = (bf16[1024,512]{1,0:T(8,128)(2,1)S(1)}, bf16[1024,512]{1,0:T(8,128)(2,1)S(1)}, u32[]{:S(2)}, u32[]{:S(2)}) collective-permute-start(bf16[1024,512]{1,0:T(8,128)(2,1)S(1)} %get-tuple-element.235), channel_id=1, source_target_pairs={{4,0},{8,4},{12,8},{16,12},{20,16},{24,20},{28,24},{5,1},{9,5},{13... | collective-permute-start | bytes 3145736 | tf_op jit(solution)/shard_map/while/body/eval_jaxpr/ppermute | solution.py:10
  274.8 16.1 %collective-permute-start = (bf16[1024,512]{1,0:T(8,128)(2,1)S(1)}, bf16[1024,512]{1,0:T(8,128)(2,1)S(1)}, u32[]{:S(2)}, u32[]{:S(2)}) collective-permute-start(bf16[1024,512]{1,0:T(8,128)(2,1)S(1)} %get-tuple-element.235), channel_id=1, source_target_pairs={{4,0},{8,4},{12,8},{16,12},{20,16},{24,20},{28,24},{5,1},{9,5},{13... | collective-permute-start | bytes 3145736 | tf_op jit(solution)/shard_map/while/body/eval_jaxpr/ppermute | solution.py:10
  291.1 16.1 %collective-permute-start = (bf16[1024,512]{1,0:T(8,128)(2,1)S(1)}, bf16[1024,512]{1,0:T(8,128)(2,1)S(1)}, u32[]{:S(2)}, u32[]{:S(2)}) collective-permute-start(bf16[1024,512]{1,0:T(8,128)(2,1)S(1)} %get-tuple-element.235), channel_id=1, source_target_pairs={{4,0},{8,4},{12,8},{16,12},{20,16},{24,20},{28,24},{5,1},{9,5},{13... | collective-permute-start | bytes 3145736 | tf_op jit(solution)/shard_map/while/body/eval_jaxpr/ppermute | solution.py:10
Sparse Core Ops, SparseCore 0:
  8.9 117.5 all-gather.1
where the time goes:
time: 315 us; the launch traced here: 314 us
  waiting for transfers between devices  265 us (84%)
  starting transfers between devices  15.8 us (5%)
  between operations  13.4 us (4%)
  local copies, waits for them, and re-layouts  8.74 us (3%)
  matrix products  8.52 us (3%)
    ppermute x8, waiting for transfers between devices, from_behind(): return lax.ppermute(block, axis, route)  145 us
    all_gather x1, waiting for transfers between devices, shards(): blocks = lax.all_gather(steps, 'space', axis=1, tiled=True)  119 us
    ppermute x8, starting transfers between devices, from_behind(): return lax.ppermute(block, axis, route)  15.8 us
    dot_general x3, matrix products, live(): value = jnp.dot(blocks[slot], carry_in, preferred_element_type=jnp.float32)  8.52 us
  transfers between devices with their start and end apart: 9, of which 9 were waited for; matrix products, arithmetic and copies ran while one was open for 0% of the time, Pallas kernels for 0%

commit v1 on v0

v1 whole, which is shorter than its diff:
```python
import functools

import jax
import jax.numpy as jnp
from jax import lax
from jax.experimental import pallas as pl
from jax.experimental.pallas import tpu as pltpu
from jax.sharding import PartitionSpec as P

MESH = pl.DeviceIdType.MESH
CHUNK = 128
TILE = 256


def kernel(
    nt, nz, len_ref, steps_ref, anchor_ref, out_ref, full, carry, gsend, grecv, csend, crecv
):
    t, z = lax.axis_index("tm"), lax.axis_index("space")
    cap, rows, nodes = steps_ref.shape
    width = anchor_ref.shape[1]
    chunk = min(CHUNK, width)
    tile = min(TILE, nodes)

    barrier = pltpu.get_barrier_semaphore()
    for axis, at, size in (("tm", t, nt), ("space", z, nz)):
        for step in (1, size - 1):
            pl.semaphore_signal(
                barrier,
                inc=1,
                device_id={axis: lax.rem(at + step, size)},
                device_id_type=MESH,
            )
    pl.semaphore_wait(barrier, 4)

    def place(slot, owner):
        return full.at[slot, pl.ds(pl.multiple_of(owner * rows, rows), rows)]

    def hop(slot, s, way):
        owner = z - way * s
        d = (1 - way) // 2
        return pltpu.make_async_remote_copy(
            src_ref=steps_ref.at[slot] if s == 0 else place(slot, owner),
            dst_ref=place(slot, owner),
            send_sem=gsend.at[d, slot, s],
            recv_sem=grecv.at[d, slot, s],
            device_id={"space": z + way},
            device_id_type=MESH,
        )

    def sends(s, way):
        if way > 0:
            return (z >= s) & (z < nz - 1)
        return (z + s < nz) & (z > 0)

    def receives(s, way):
        return z - 1 >= s if way > 0 else z + 1 + s < nz

    def arrival(slot, s, way):
        owner = z - way * (s + 1)
        d = (1 - way) // 2
        return pltpu.make_async_remote_copy(
            src_ref=place(slot, owner),
            dst_ref=place(slot, owner),
            send_sem=gsend.at[d, slot, s],
            recv_sem=grecv.at[d, slot, s],
            device_id={"space": z - way},
            device_id_type=MESH,
        )

    def launch(slot, s):
        for way in (1, -1):

            @pl.when(sends(s, way))
            def _():
                hop(slot, s, way).start()

    order = list(range(cap - 1, -1, -1))
    launch(order[0], 0)
    for i, slot in enumerate(order):
        if i + 1 < cap:
            launch(order[i + 1], 0)
        place(slot, z)[...] = steps_ref[slot]
        for s in range(nz - 1):
            for way in (1, -1):

                @pl.when(receives(s, way))
                def _():
                    arrival(slot, s, way).wait_recv()

                if s + 1 < nz - 1:

                    @pl.when(sends(s + 1, way))
                    def _():
                        hop(slot, s + 1, way).start()

    @pl.when(t == nt - 1)
    def _():
        carry[...] = anchor_ref[...]

    def pass_on(k, device):
        columns = pl.ds(pl.multiple_of(k * chunk, chunk), chunk)
        return pltpu.make_async_remote_copy(
            src_ref=out_ref.at[0, :, columns],
            dst_ref=carry.at[:, columns],
            send_sem=csend.at[k],
            recv_sem=crecv.at[k],
            device_id={"tm": device},
            device_id_type=MESH,
        )

    length = len_ref[0]

    def one_chunk(k, _):
        columns = pl.ds(pl.multiple_of(k * chunk, chunk), chunk)

        @pl.when(t < nt - 1)
        def _():
            pass_on(k, t + 1).wait_recv()

        for slot in order:
            before = carry.at[:, columns] if slot == cap - 1 else out_ref.at[slot + 1, :, columns]
            operand = before[...]
            for r in range(0, nodes, tile):
                value = jnp.dot(
                    full[slot, r : r + tile, :], operand, preferred_element_type=jnp.float32
                )
                kept = before[r : r + tile, :].astype(jnp.float32)
                value = jnp.where(slot < length, value, kept)
                out_ref[slot, r : r + tile, columns] = value.astype(out_ref.dtype)

        @pl.when(t > 0)
        def _():
            pass_on(k, t - 1).start()

        return 0

    lax.fori_loop(0, width // chunk, one_chunk, 0)

    for slot in order:
        for s in range(nz - 1):
            for way in (1, -1):

                @pl.when(sends(s, way))
                def _():
                    hop(slot, s, way).wait_send()

    @pl.when(t > 0)
    def _():
        for k in range(width // chunk):
            pass_on(k, t - 1).wait_send()


def shards(nt, nz, steps, lengths, anchor):
    cap, rows, nodes = steps.shape
    width = anchor.shape[1]
    chunks = width // min(CHUNK, width)
    vmem = pl.BlockSpec(memory_space=pltpu.VMEM)
    panels = pl.pallas_call(
        functools.partial(kernel, nt, nz),
        out_shape=jax.ShapeDtypeStruct((cap, nodes, width), jnp.bfloat16),
        in_specs=[pl.BlockSpec(memory_space=pltpu.SMEM), vmem, vmem],
        out_specs=vmem,
        scratch_shapes=[
            pltpu.VMEM((cap, nodes, nodes), jnp.bfloat16),
            pltpu.VMEM((nodes, width), jnp.bfloat16),
            pltpu.SemaphoreType.DMA((2, cap, nz - 1)),
            pltpu.SemaphoreType.DMA((2, cap, nz - 1)),
            pltpu.SemaphoreType.DMA((chunks,)),
            pltpu.SemaphoreType.DMA((chunks,)),
        ],
        compiler_params=pltpu.CompilerParams(collective_id=0, has_side_effects=True),
    )(lengths, steps, anchor)
    used = jnp.arange(cap) < lengths[0]
    return jnp.where(used[:, None, None], panels.astype(jnp.float32), 0.0)


def solution(mesh):
    return jax.shard_map(
        functools.partial(shards, mesh.shape["tm"], mesh.shape["space"]),
        mesh=mesh,
        in_specs=(P("tm", "space", None), P("tm"), P(None, "space")),
        out_specs=P("tm", None, "space"),
        check_vma=False,
    )
```

time: 315 us -> 162 us (0.51)
  the two profiles are of different devices: /device:TPU:1 before, /device:TPU:0 now
where the time goes in v1:
time: 162 us
  Pallas kernels  156 us (96%)
  other arithmetic  5.59 us (3%)
    pallas_call x1, Pallas kernels, shards(): pl.pallas_call(functools.partial(kernel, nt, nz), out_shape=jax.ShapeDtyp...  156 us
    select_n x1, other arithmetic, shards(): return jnp.where(used[:, None, None], panels.astype(jnp.float32), 0.0)  5.59 us

profile of v1, /device:TPU:0, one launch (start us, length us, event | category | flops | bytes accessed | tf_op | source)
XLA Modules:
  0.0 161.8 jit_solution(5999135558642272344)
XLA Ops:
  0.7 155.5 %shard_map.37 = bf16[3,1024,512]{2,1,0:T(8,128)(2,1)} custom-call(s32[1]{0:T(128)} %copy.4.len_ref, bf16[3,256,1024]{2,1,0:T(8,128)(2,1)} %steps_ref.1, bf16[1024,512]{1,0:T(8,128)(2,1)} %anchor_ref.1), custom_call_target="tpu_custom_call" | custom-call | tf_op jit(solution)/shard_map/pallas_call | solution.py:158
  156.2 5.6 %convert_select_fusion = f32[3,1024,512]{2,1,0:T(8,128)} fusion(bf16[3,1024,512]{2,1,0:T(8,128)(2,1)} %shard_map.37, pred[3]{0:T(512)(128)(4,1)S(1)} %iota_compare_fusion), kind=kLoop, calls=%fused_computation | loop fusion | flops 3145728 | bytes 9437187 | tf_op jit(solution)/shard_map/jit(_where)/select_n | solution.py:174
  (1 shorter events, 0.0 us)

commit v2 on v1

--- a/solution.py
+++ b/solution.py
@@ -13,7 +13,8 @@
 
 
 def kernel(
-    nt, nz, len_ref, steps_ref, anchor_ref, out_ref, full, carry, gsend, grecv, csend, crecv
+    nt, nz, len_ref, steps_ref, anchor_ref, out_ref, full, carry, scout_out, scout_in,
+    gsend, grecv, csend, crecv, ssend, srecv, asend
 ):
     t, z = lax.axis_index("tm"), lax.axis_index("space")
     cap, rows, nodes = steps_ref.shape
@@ -30,7 +31,53 @@
                 device_id={axis: lax.rem(at + step, size)},
                 device_id_type=MESH,
             )
-    pl.semaphore_wait(barrier, 4)
+    half = nt // 2
+    at_end = (z == 0) | (z == nz - 1)
+    scouts = (z == 1) | (z == nz - 2)
+    end = jnp.where(z <= 1, 0, nz - 1)
+    scout = jnp.where(z <= 1, 1, nz - 2)
+    gives, takes = scouts & (t == half), at_end & (t == half - 1)
+
+    @pl.when(gives)
+    def _():
+        pl.semaphore_signal(
+            barrier,
+            inc=1,
+            device_id={"tm": half - 1, "space": end},
+            device_id_type=MESH,
+        )
+
+    @pl.when(takes)
+    def _():
+        pl.semaphore_signal(
+            barrier,
+            inc=1,
+            device_id={"tm": half, "space": scout},
+            device_id_type=MESH,
+        )
+
+    pl.semaphore_wait(barrier, 4 + jnp.where(gives | takes, 1, 0))
+
+    def stripe(k):
+        return pl.ds(pl.multiple_of(k * chunk, chunk), chunk)
+
+    def lend(k, device):
+        return pltpu.make_async_remote_copy(
+            src_ref=anchor_ref.at[:, stripe(k)],
+            dst_ref=scout_in.at[:, stripe(k)],
+            send_sem=asend.at[k],
+            recv_sem=srecv.at[k],
+            device_id={"space": device},
+            device_id_type=MESH,
+        )
+
+    lends = at_end & (t == nt - 1)
+    chunks = width // chunk
+
+    @pl.when(lends)
+    def _():
+        for k in range(chunks):
+            lend(k, scout).start()
 
     def place(slot, owner):
         return full.at[slot, pl.ds(pl.multiple_of(owner * rows, rows), rows)]
@@ -98,27 +145,41 @@
         carry[...] = anchor_ref[...]
 
     def pass_on(k, device):
-        columns = pl.ds(pl.multiple_of(k * chunk, chunk), chunk)
-        return pltpu.make_async_remote_copy(
-            src_ref=out_ref.at[0, :, columns],
-            dst_ref=carry.at[:, columns],
+        return pltpu.make_async_remote_copy(
+            src_ref=out_ref.at[0, :, stripe(k)],
+            dst_ref=carry.at[:, stripe(k)],
             send_sem=csend.at[k],
             recv_sem=crecv.at[k],
             device_id={"tm": device},
             device_id_type=MESH,
         )
 
+    def scout_on(k, device):
+        return pltpu.make_async_remote_copy(
+            src_ref=scout_out.at[0, :, stripe(k)],
+            dst_ref=scout_in.at[:, stripe(k)],
+            send_sem=ssend.at[k],
+            recv_sem=srecv.at[k],
+            device_id={"tm": device},
+            device_id_type=MESH,
+        )
+
+    def hand_over(k):
+        return pltpu.make_async_remote_copy(
+            src_ref=scout_out.at[0, :, stripe(k)],
+            dst_ref=carry.at[:, stripe(k)],
+            send_sem=ssend.at[k],
+            recv_sem=crecv.at[k],
+            device_id={"tm": half - 1, "space": end},
+            device_id_type=MESH,
+        )
+
     length = len_ref[0]
 
-    def one_chunk(k, _):
-        columns = pl.ds(pl.multiple_of(k * chunk, chunk), chunk)
-
-        @pl.when(t < nt - 1)
-        def _():
-            pass_on(k, t + 1).wait_recv()
-
+    def days(k, source, result):
+        columns = stripe(k)
         for slot in order:
-            before = carry.at[:, columns] if slot == cap - 1 else out_ref.at[slot + 1, :, columns]
+            before = source.at[:, columns] if slot == cap - 1 else result.at[slot + 1, :, columns]
             operand = before[...]
             for r in range(0, nodes, tile):
                 value = jnp.dot(
@@ -126,15 +187,57 @@
                 )
                 kept = before[r : r + tile, :].astype(jnp.float32)
                 value = jnp.where(slot < length, value, kept)
-                out_ref[slot, r : r + tile, columns] = value.astype(out_ref.dtype)
-
-        @pl.when(t > 0)
+                result[slot, r : r + tile, columns] = value.astype(result.dtype)
+
+    @pl.when(scouts & (t >= half))
+    def _():
+        def scout_chunk(k, _):
+            scout_on(k, t - 1).wait_recv()
+            days(k, scout_in, scout_out)
+
+            @pl.when(t > half)
+            def _():
+                scout_on(k, t - 1).start()
+
+            @pl.when(t == half)
+            def _():
+                hand_over(k).start()
+
+            return 0
+
+        lax.fori_loop(0, chunks, scout_chunk, 0)
+
+    passes = (t > 0) & jnp.logical_not(at_end & (t == half))
+
+    def one_chunk(k, _):
+        @pl.when(t < nt - 1)
+        def _():
+            pass_on(k, t + 1).wait_recv()
+
+        days(k, carry, out_ref)
+
+        @pl.when(passes)
         def _():
             pass_on(k, t - 1).start()
 
         return 0
 
-    lax.fori_loop(0, width // chunk, one_chunk, 0)
+    lax.fori_loop(0, chunks, one_chunk, 0)
+
+    @pl.when(lends)
+    def _():
+        for k in range(chunks):
+            lend(k, scout).wait_send()
+
+    @pl.when(scouts & (t > half))
+    def _():
+        for k in range(chunks):
+            scout_on(k, t - 1).wait_send()
+
+    @pl.when(gives)
+    def _():
+        for k in range(chunks):
+            hand_over(k).wait_send()
 
     for slot in order:
         for s in range(nz - 1):
@@ -144,9 +247,9 @@
                 def _():
                     hop(slot, s, way).wait_send()
 
-    @pl.when(t > 0)
-    def _():
-        for k in range(width // chunk):
+    @pl.when(passes)
+    def _():
+        for k in range(chunks):
             pass_on(k, t - 1).wait_send()
 
 
@@ -163,8 +266,13 @@
         scratch_shapes=[
             pltpu.VMEM((cap, nodes, nodes), jnp.bfloat16),
             pltpu.VMEM((nodes, width), jnp.bfloat16),
+            pltpu.VMEM((cap, nodes, width), jnp.bfloat16),
+            pltpu.VMEM((nodes, width), jnp.bfloat16),
             pltpu.SemaphoreType.DMA((2, cap, nz - 1)),
             pltpu.SemaphoreType.DMA((2, cap, nz - 1)),
+            pltpu.SemaphoreType.DMA((chunks,)),
+            pltpu.SemaphoreType.DMA((chunks,)),
+            pltpu.SemaphoreType.DMA((chunks,)),
             pltpu.SemaphoreType.DMA((chunks,)),
             pltpu.SemaphoreType.DMA((chunks,)),
         ],

time: 162 us -> 146 us (0.901)
  Pallas kernels: 156 us -> 140 us
    pallas_call x1, Pallas kernels: 156 us -> 140 us  [shards(): pl.pallas_call(functools.partial(kernel, nt, nz), out_shape=jax.ShapeDtyp...]
where the time goes in v2:
time: 146 us
  Pallas kernels  140 us (96%)
  other arithmetic  5.59 us (4%)
    pallas_call x1, Pallas kernels, shards(): pl.pallas_call(functools.partial(kernel, nt, nz), out_shape=jax.ShapeDtyp...  140 us
    select_n x1, other arithmetic, shards(): return jnp.where(used[:, None, None], panels.astype(jnp.float32), 0.0)  5.59 us

profile of v2, /device:TPU:0, one launch (start us, length us, event | category | flops | bytes accessed | tf_op | source)
XLA Modules:
  0.0 146.3 jit_solution(12822630661362267350)
XLA Ops:
  0.7 140.0 %shard_map.37 = bf16[3,1024,512]{2,1,0:T(8,128)(2,1)} custom-call(s32[1]{0:T(128)} %copy.4.len_ref, bf16[3,256,1024]{2,1,0:T(8,128)(2,1)} %steps_ref.1, bf16[1024,512]{1,0:T(8,128)(2,1)} %anchor_ref.1), custom_call_target="tpu_custom_call" | custom-call | tf_op jit(solution)/shard_map/pallas_call | solution.py:261
  140.7 5.6 %convert_select_fusion = f32[3,1024,512]{2,1,0:T(8,128)} fusion(bf16[3,1024,512]{2,1,0:T(8,128)(2,1)} %shard_map.37, pred[3]{0:T(512)(128)(4,1)S(1)} %iota_compare_fusion), kind=kLoop, calls=%fused_computation | loop fusion | flops 3145728 | bytes 9437187 | tf_op jit(solution)/shard_map/jit(_where)/select_n | solution.py:282
  (1 shorter events, 0.0 us)

commit v3 on v2

v3 whole, which is shorter than its diff:
```python
import functools

import jax
import jax.numpy as jnp
from jax import lax
from jax.experimental import pallas as pl
from jax.experimental.pallas import tpu as pltpu
from jax.sharding import PartitionSpec as P

MESH = pl.DeviceIdType.MESH
CHUNK = 128
TILE = 256
SPANS = 2


def kernel(
    nt, nz, len_ref, steps_ref, anchor_ref, out_ref, full, carry, scout_out, scout_in,
    gsend, grecv, csend, crecv, ssend, srecv, asend, hsend
):
    t, z = lax.axis_index("tm"), lax.axis_index("space")
    cap, rows, nodes = steps_ref.shape
    width = anchor_ref.shape[1]
    chunk = min(CHUNK, width)
    tile = min(TILE, nodes)

    barrier = pltpu.get_barrier_semaphore()
    for axis, at, size in (("tm", t, nt), ("space", z, nz)):
        for step in (1, size - 1):
            pl.semaphore_signal(
                barrier,
                inc=1,
                device_id={axis: lax.rem(at + step, size)},
                device_id_type=MESH,
            )
    span = nt // SPANS
    at_end = (z == 0) | (z == nz - 1)
    scouts = (z == 1) | (z == nz - 2)
    end = jnp.where(z <= 1, 0, nz - 1)
    scout = jnp.where(z <= 1, 1, nz - 2)
    edge = lax.rem(t, span) == 0
    gives = scouts & edge & (t > 0)
    takes = at_end & (lax.rem(t, span) == span - 1) & (t < nt - 1)

    @pl.when(gives)
    def _():
        pl.semaphore_signal(
            barrier,
            inc=1,
            device_id={"tm": t - 1, "space": end},
            device_id_type=MESH,
        )

    @pl.when(takes)
    def _():
        pl.semaphore_signal(
            barrier,
            inc=1,
            device_id={"tm": t + 1, "space": scout},
            device_id_type=MESH,
        )

    pl.semaphore_wait(barrier, 4 + jnp.where(gives | takes, 1, 0))

    def stripe(k):
        return pl.ds(pl.multiple_of(k * chunk, chunk), chunk)

    def lend(k, device):
        return pltpu.make_async_remote_copy(
            src_ref=anchor_ref.at[:, stripe(k)],
            dst_ref=scout_in.at[:, stripe(k)],
            send_sem=asend.at[k],
            recv_sem=srecv.at[k],
            device_id={"space": device},
            device_id_type=MESH,
        )

    lends = at_end & (t == nt - 1)
    chunks = width // chunk

    @pl.when(lends)
    def _():
        for k in range(chunks):
            lend(k, scout).start()

    order = list(range(cap - 1, -1, -1))
    length = len_ref[0]
    pair = 2 if chunks % 2 == 0 else 1

    def days(k, count, source, result, slots):
        columns = pl.ds(pl.multiple_of(k * chunk, chunk), count * chunk)
        for slot in slots:
            before = source.at[:, columns] if slot == cap - 1 else result.at[slot + 1, :, columns]
            operand = before[...]
            for r in range(0, nodes, tile):
                value = jnp.dot(
                    full[slot, r : r + tile, :], operand, preferred_element_type=jnp.float32
                )
                kept = before[r : r + tile, :].astype(jnp.float32)
                value = jnp.where(slot < length, value, kept)
                result[slot, r : r + tile, columns] = value.astype(result.dtype)

    @pl.when(t == nt - 1)
    def _():
        carry[...] = anchor_ref[...]

    def place(slot, owner):
        return full.at[slot, pl.ds(pl.multiple_of(owner * rows, rows), rows)]

    def hop(slot, s, way):
        owner = z - way * s
        d = (1 - way) // 2
        return pltpu.make_async_remote_copy(
            src_ref=steps_ref.at[slot] if s == 0 else place(slot, owner),
            dst_ref=place(slot, owner),
            send_sem=gsend.at[d, slot, s],
            recv_sem=grecv.at[d, slot, s],
            device_id={"space": z + way},
            device_id_type=MESH,
        )

    def sends(s, way):
        if way > 0:
            return (z >= s) & (z < nz - 1)
        return (z + s < nz) & (z > 0)

    def receives(s, way):
        return z - 1 >= s if way > 0 else z + 1 + s < nz

    def arrival(slot, s, way):
        owner = z - way * (s + 1)
        d = (1 - way) // 2
        return pltpu.make_async_remote_copy(
            src_ref=place(slot, owner),
            dst_ref=place(slot, owner),
            send_sem=gsend.at[d, slot, s],
            recv_sem=grecv.at[d, slot, s],
            device_id={"space": z - way},
            device_id_type=MESH,
        )

    def launch(slot, s):
        for way in (1, -1):

            @pl.when(sends(s, way))
            def _():
                hop(slot, s, way).start()

    launch(order[0], 0)
    for i, slot in enumerate(order):
        if i + 1 < cap:
            launch(order[i + 1], 0)
        place(slot, z)[...] = steps_ref[slot]
        for s in range(nz - 1):
            for way in (1, -1):

                @pl.when(receives(s, way))
                def _():
                    arrival(slot, s, way).wait_recv()

                if s + 1 < nz - 1:

                    @pl.when(sends(s + 1, way))
                    def _():
                        hop(slot, s + 1, way).start()

        if slot > 0:
            @pl.when(t == nt - 1)
            def _():
                def early(k, _):
                    days(k * pair, pair, carry, out_ref, [slot])
                    return 0

                lax.fori_loop(0, chunks // pair, early, 0)

    def pass_on(k, device):
        return pltpu.make_async_remote_copy(
            src_ref=out_ref.at[0, :, stripe(k)],
            dst_ref=carry.at[:, stripe(k)],
            send_sem=csend.at[k],
            recv_sem=crecv.at[k],
            device_id={"tm": device},
            device_id_type=MESH,
        )

    def scout_on(k, device):
        return pltpu.make_async_remote_copy(
            src_ref=scout_out.at[0, :, stripe(k)],
            dst_ref=scout_in.at[:, stripe(k)],
            send_sem=ssend.at[k],
            recv_sem=srecv.at[k],
            device_id={"tm": device},
            device_id_type=MESH,
        )

    def hand_over(k):
        return pltpu.make_async_remote_copy(
            src_ref=scout_out.at[0, :, stripe(k)],
            dst_ref=carry.at[:, stripe(k)],
            send_sem=hsend.at[k],
            recv_sem=crecv.at[k],
            device_id={"tm": t - 1, "space": end},
            device_id_type=MESH,
        )

    @pl.when(scouts & (t >= span))
    def _():
        def scout_chunk(j, _):
            for k in range(pair):
                scout_on(j * pair + k, t - 1).wait_recv()
            days(j * pair, pair, scout_in, scout_out, order)
            for k in range(pair):

                @pl.when(edge)
                def _():
                    hand_over(j * pair + k).start()

                @pl.when(t > span)
                def _():
                    scout_on(j * pair + k, t - 1).start()

            return 0

        lax.fori_loop(0, chunks // pair, scout_chunk, 0)

    passes = (t > 0) & jnp.logical_not(at_end & edge)

    def chain(count):
        def one_chunk(j, _):
            @pl.when(t < nt - 1)
            def _():
                for k in range(count):
                    pass_on(j * count + k, t + 1).wait_recv()
                days(j * count, count, carry, out_ref, order)

            @pl.when(t == nt - 1)
            def _():
                days(j * count, count, carry, out_ref, order[-1:])

            @pl.when(passes)
            def _():
                for k in range(count):
                    pass_on(j * count + k, t - 1).start()

            return 0

        lax.fori_loop(0, chunks // count, one_chunk, 0)

    @pl.when(at_end)
    def _():
        chain(1)

    @pl.when(jnp.logical_not(at_end))
    def _():
        chain(pair)

    @pl.when(lends)
    def _():
        for k in range(chunks):
            lend(k, scout).wait_send()

    @pl.when(scouts & (t > span))
    def _():
        for k in range(chunks):
            scout_on(k, t - 1).wait_send()

    @pl.when(gives)
    def _():
        for k in range(chunks):
            hand_over(k).wait_send()

    for slot in order:
        for s in range(nz - 1):
            for way in (1, -1):

                @pl.when(sends(s, way))
                def _():
                    hop(slot, s, way).wait_send()

    @pl.when(passes)
    def _():
        for k in range(chunks):
            pass_on(k, t - 1).wait_send()


def shards(nt, nz, steps, lengths, anchor):
    cap, rows, nodes = steps.shape
    width = anchor.shape[1]
    chunks = width // min(CHUNK, width)
    vmem = pl.BlockSpec(memory_space=pltpu.VMEM)
    panels = pl.pallas_call(
        functools.partial(kernel, nt, nz),
        out_shape=jax.ShapeDtypeStruct((cap, nodes, width), jnp.bfloat16),
        in_specs=[pl.BlockSpec(memory_space=pltpu.SMEM), vmem, vmem],
        out_specs=vmem,
        scratch_shapes=[
            pltpu.VMEM((cap, nodes, nodes), jnp.bfloat16),
            pltpu.VMEM((nodes, width), jnp.bfloat16),
            pltpu.VMEM((cap, nodes, width), jnp.bfloat16),
            pltpu.VMEM((nodes, width), jnp.bfloat16),
            pltpu.SemaphoreType.DMA((2, cap, nz - 1)),
            pltpu.SemaphoreType.DMA((2, cap, nz - 1)),
            pltpu.SemaphoreType.DMA((chunks,)),
            pltpu.SemaphoreType.DMA((chunks,)),
            pltpu.SemaphoreType.DMA((chunks,)),
            pltpu.SemaphoreType.DMA((chunks,)),
            pltpu.SemaphoreType.DMA((chunks,)),
            pltpu.SemaphoreType.DMA((chunks,)),
        ],
        compiler_params=pltpu.CompilerParams(collective_id=0, has_side_effects=True),
    )(lengths, steps, anchor)
    used = jnp.arange(cap) < lengths[0]
    return jnp.where(used[:, None, None], panels.astype(jnp.float32), 0.0)


def solution(mesh):
    return jax.shard_map(
        functools.partial(shards, mesh.shape["tm"], mesh.shape["space"]),
        mesh=mesh,
        in_specs=(P("tm", "space", None), P("tm"), P(None, "space")),
        out_specs=P("tm", None, "space"),
        check_vma=False,
    )
```

time: 146 us -> 150 us (1.027)
  the two profiles are of different devices: /device:TPU:0 before, /device:TPU:8 now
where the time goes in v3:
time: 150 us; the launch traced here: 149 us
  Pallas kernels  143 us (95%)
  other arithmetic  5.59 us (4%)
    pallas_call x1, Pallas kernels, shards(): pl.pallas_call(functools.partial(kernel, nt, nz), out_shape=jax.ShapeDtyp...  143 us
    select_n x1, other arithmetic, shards(): return jnp.where(used[:, None, None], panels.astype(jnp.float32), 0.0)  5.59 us

profile of v3, /device:TPU:8, one launch (start us, length us, event | category | flops | bytes accessed | tf_op | source)
XLA Modules:
  0.0 149.4 jit_solution(5168967377813633488)
XLA Ops:
  0.7 143.1 %shard_map.37 = bf16[3,1024,512]{2,1,0:T(8,128)(2,1)} custom-call(s32[1]{0:T(128)} %copy.4.len_ref, bf16[3,256,1024]{2,1,0:T(8,128)(2,1)} %steps_ref.1, bf16[1024,512]{1,0:T(8,128)(2,1)} %anchor_ref.1), custom_call_target="tpu_custom_call" | custom-call | tf_op jit(solution)/shard_map/pallas_call | solution.py:290
  143.8 5.6 %convert_select_fusion = f32[3,1024,512]{2,1,0:T(8,128)} fusion(bf16[3,1024,512]{2,1,0:T(8,128)(2,1)} %shard_map.37, pred[3]{0:T(512)(128)(4,1)S(1)} %iota_compare_fusion), kind=kLoop, calls=%fused_computation | loop fusion | flops 3145728 | bytes 9437187 | tf_op jit(solution)/shard_map/jit(_where)/select_n | solution.py:312
  (1 shorter events, 0.0 us)

commit v4 on v3

--- a/solution.py
+++ b/solution.py
@@ -10,7 +10,7 @@
 MESH = pl.DeviceIdType.MESH
 CHUNK = 128
 TILE = 256
-SPANS = 2
+SPANS = 4
 
 
 def kernel(
@@ -32,7 +32,7 @@
                 device_id={axis: lax.rem(at + step, size)},
                 device_id_type=MESH,
             )
-    span = nt // SPANS
+    span = max(1, nt // SPANS)
     at_end = (z == 0) | (z == nz - 1)
     scouts = (z == 1) | (z == nz - 2)
     end = jnp.where(z <= 1, 0, nz - 1)
@@ -204,23 +204,21 @@
 
     @pl.when(scouts & (t >= span))
     def _():
-        def scout_chunk(j, _):
-            for k in range(pair):
-                scout_on(j * pair + k, t - 1).wait_recv()
-            days(j * pair, pair, scout_in, scout_out, order)
-            for k in range(pair):
-
-                @pl.when(edge)
-                def _():
-                    hand_over(j * pair + k).start()
-
-                @pl.when(t > span)
-                def _():
-                    scout_on(j * pair + k, t - 1).start()
+        def scout_chunk(k, _):
+            scout_on(k, t - 1).wait_recv()
+            days(k, 1, scout_in, scout_out, order)
+
+            @pl.when(edge)
+            def _():
+                hand_over(k).start()
+
+            @pl.when(t > span)
+            def _():
+                scout_on(k, t - 1).start()
 
             return 0
 
-        lax.fori_loop(0, chunks // pair, scout_chunk, 0)
+        lax.fori_loop(0, chunks, scout_chunk, 0)
 
     passes = (t > 0) & jnp.logical_not(at_end & edge)
 
@@ -247,11 +245,11 @@
 
     @pl.when(at_end)
     def _():
+        chain(pair)
+
+    @pl.when(jnp.logical_not(at_end))
+    def _():
         chain(1)
-
-    @pl.when(jnp.logical_not(at_end))
-    def _():
-        chain(pair)
 
     @pl.when(lends)
     def _():

time: 150 us -> 144 us (0.960)
  Pallas kernels: 143 us -> 138 us
    pallas_call x1, Pallas kernels: 143 us -> 138 us  [shards(): pl.pallas_call(functools.partial(kernel, nt, nz), out_shape=jax.ShapeDtyp...]
where the time goes in v4:
time: 144 us
  Pallas kernels  138 us (96%)
  other arithmetic  5.59 us (4%)
    pallas_call x1, Pallas kernels, shards(): pl.pallas_call(functools.partial(kernel, nt, nz), out_shape=jax.ShapeDtyp...  138 us
    select_n x1, other arithmetic, shards(): return jnp.where(used[:, None, None], panels.astype(jnp.float32), 0.0)  5.59 us

profile of v4, /device:TPU:8, one launch (start us, length us, event | category | flops | bytes accessed | tf_op | source)
XLA Modules:
  0.0 143.8 jit_solution(5653338110412954673)
XLA Ops:
  0.7 137.5 %shard_map.37 = bf16[3,1024,512]{2,1,0:T(8,128)(2,1)} custom-call(s32[1]{0:T(128)} %copy.4.len_ref, bf16[3,256,1024]{2,1,0:T(8,128)(2,1)} %steps_ref.1, bf16[1024,512]{1,0:T(8,128)(2,1)} %anchor_ref.1), custom_call_target="tpu_custom_call" | custom-call | tf_op jit(solution)/shard_map/pallas_call | solution.py:288
  138.2 5.6 %convert_select_fusion = f32[3,1024,512]{2,1,0:T(8,128)} fusion(bf16[3,1024,512]{2,1,0:T(8,128)(2,1)} %shard_map.37, pred[3]{0:T(512)(128)(4,1)S(1)} %iota_compare_fusion), kind=kLoop, calls=%fused_computation | loop fusion | flops 3145728 | bytes 9437187 | tf_op jit(solution)/shard_map/jit(_where)/select_n | solution.py:310
  (1 shorter events, 0.0 us)

commit v5 on v4

--- a/solution.py
+++ b/solution.py
@@ -164,7 +164,7 @@
                         hop(slot, s + 1, way).start()
 
         if slot > 0:
-            @pl.when(t == nt - 1)
+            @pl.when(at_end & (t == nt - 1))
             def _():
                 def early(k, _):
                     days(k * pair, pair, carry, out_ref, [slot])
@@ -202,11 +202,37 @@
             device_id_type=MESH,
         )
 
-    @pl.when(scouts & (t >= span))
+    def both_days(k):
+        columns = stripe(k)
+        for slot in order:
+            if slot == cap - 1:
+                mine, other = carry.at[:, columns], scout_in.at[:, columns]
+            else:
+                mine = out_ref.at[slot + 1, :, columns]
+                other = scout_out.at[slot + 1, :, columns]
+            operand = jnp.concatenate([mine[...], other[...]], axis=1)
+            for r in range(0, nodes, tile):
+                values = jnp.dot(
+                    full[slot, r : r + tile, :], operand, preferred_element_type=jnp.float32
+                )
+                for i, (before, result) in enumerate(((mine, out_ref), (other, scout_out))):
+                    value = values[:, i * chunk : (i + 1) * chunk]
+                    kept = before[r : r + tile, :].astype(jnp.float32)
+                    value = jnp.where(slot < length, value, kept)
+                    result[slot, r : r + tile, columns] = value.astype(result.dtype)
+
+    leads = scouts & (t >= span)
+
+    @pl.when(leads)
     def _():
         def scout_chunk(k, _):
+            @pl.when(t < nt - 1)
+            def _():
+                pass_on(k, t + 1).wait_recv()
+
             scout_on(k, t - 1).wait_recv()
-            days(k, 1, scout_in, scout_out, order)
+            both_days(k)
+            pass_on(k, t - 1).start()
 
             @pl.when(edge)
             def _():
@@ -228,9 +254,12 @@
             def _():
                 for k in range(count):
                     pass_on(j * count + k, t + 1).wait_recv()
+
+            @pl.when(jnp.logical_not(at_end & (t == nt - 1)))
+            def _():
                 days(j * count, count, carry, out_ref, order)
 
-            @pl.when(t == nt - 1)
+            @pl.when(at_end & (t == nt - 1))
             def _():
                 days(j * count, count, carry, out_ref, order[-1:])
 
@@ -247,7 +276,7 @@
     def _():
         chain(pair)
 
-    @pl.when(jnp.logical_not(at_end))
+    @pl.when(jnp.logical_not(at_end | leads))
     def _():
         chain(1)
 

time: 144 us -> 148 us (1.028); the launches traced: 144 us -> 146 us
    pallas_call x1, Pallas kernels: 138 us -> 139 us  [shards(): pl.pallas_call(functools.partial(kernel, nt, nz), out_shape=jax.ShapeDtyp...]
where the time goes in v5:
time: 148 us; the launch traced here: 146 us
  Pallas kernels  139 us (94%)
  other arithmetic  5.59 us (4%)
    pallas_call x1, Pallas kernels, shards(): pl.pallas_call(functools.partial(kernel, nt, nz), out_shape=jax.ShapeDtyp...  139 us
    select_n x1, other arithmetic, shards(): return jnp.where(used[:, None, None], panels.astype(jnp.float32), 0.0)  5.59 us

profile of v5, /device:TPU:8, one launch (start us, length us, event | category | flops | bytes accessed | tf_op | source)
XLA Modules:
  0.0 145.6 jit_solution(16458920700505823879)
XLA Ops:
  0.7 139.3 %shard_map.37 = bf16[3,1024,512]{2,1,0:T(8,128)(2,1)} custom-call(s32[1]{0:T(128)} %copy.4.len_ref, bf16[3,256,1024]{2,1,0:T(8,128)(2,1)} %steps_ref.1, bf16[1024,512]{1,0:T(8,128)(2,1)} %anchor_ref.1), custom_call_target="tpu_custom_call" | custom-call | tf_op jit(solution)/shard_map/pallas_call | solution.py:317
  140.0 5.6 %convert_select_fusion = f32[3,1024,512]{2,1,0:T(8,128)} fusion(bf16[3,1024,512]{2,1,0:T(8,128)(2,1)} %shard_map.37, pred[3]{0:T(512)(128)(4,1)S(1)} %iota_compare_fusion), kind=kLoop, calls=%fused_computation | loop fusion | flops 3145728 | bytes 9437187 | tf_op jit(solution)/shard_map/jit(_where)/select_n | solution.py:339
  (1 shorter events, 0.0 us)

commit v6 on v4

--- a/solution.py
+++ b/solution.py
@@ -11,6 +11,7 @@
 CHUNK = 128
 TILE = 256
 SPANS = 4
+GRANT = 28 << 20
 
 
 def kernel(
@@ -304,7 +305,9 @@
             pltpu.SemaphoreType.DMA((chunks,)),
             pltpu.SemaphoreType.DMA((chunks,)),
         ],
-        compiler_params=pltpu.CompilerParams(collective_id=0, has_side_effects=True),
+        compiler_params=pltpu.CompilerParams(
+            collective_id=0, has_side_effects=True, vmem_limit_bytes=GRANT
+        ),
     )(lengths, steps, anchor)
     used = jnp.arange(cap) < lengths[0]
     return jnp.where(used[:, None, None], panels.astype(jnp.float32), 0.0)

time: 144 us -> 141 us (0.979)
  Pallas kernels: 138 us -> 134 us
  local copies, waits for them, and re-layouts: 0 us -> 2.63 us
  other arithmetic: 5.59 us -> 3.7 us
    pallas_call x1, Pallas kernels: 138 us -> 134 us  [shards(): pl.pallas_call(functools.partial(kernel, nt, nz), out_shape=jax.ShapeDtyp...]
    unnamed x0 -> x4, local copies, waits for them, and re-layouts: none -> 2.63 us
    select_n x1, other arithmetic: 5.59 us -> 3.7 us  [shards(): return jnp.where(used[:, None, None], panels.astype(jnp.float32), 0.0)]
where the time goes in v6:
time: 141 us
  Pallas kernels  134 us (95%)
  other arithmetic  3.7 us (3%)
  local copies, waits for them, and re-layouts  2.63 us (2%)
    pallas_call x1, Pallas kernels, shards(): pl.pallas_call(functools.partial(kernel, nt, nz), out_shape=jax.ShapeDtyp...  134 us
    select_n x1, other arithmetic, shards(): return jnp.where(used[:, None, None], panels.astype(jnp.float32), 0.0)  3.7 us

profile of v6, /device:TPU:8, one launch (start us, length us, event | category | flops | bytes accessed | tf_op | source)
XLA Modules:
  0.0 141.1 jit_solution(3569918684697380119)
XLA Ops:
  0.7 0.0 copy-start
  0.7 1.4 copy-done
  2.1 0.0 copy-start.1
  2.1 1.2 copy-done.1
  3.3 134.1 %shard_map.37 = bf16[3,1024,512]{2,1,0:T(8,128)(2,1)S(1)} custom-call(s32[1]{0:T(128)} %copy.4.len_ref, bf16[3,256,1024]{2,1,0:T(8,128)(2,1)S(1)} %copy-done, bf16[1024,512]{1,0:T(8,128)(2,1)S(1)} %copy-done.1), custom_call_target="tpu_custom_call" | custom-call | tf_op jit(solution)/shard_map/pallas_call | solution.py:289
  137.4 3.7 %convert_select_fusion = f32[3,1024,512]{2,1,0:T(8,128)} fusion(bf16[3,1024,512]{2,1,0:T(8,128)(2,1)S(1)} %shard_map.37, pred[3]{0:T(512)(128)(4,1)S(1)} %iota_compare_fusion), kind=kLoop, calls=%fused_computation | loop fusion | flops 3145728 | bytes 9437187 | tf_op jit(solution)/shard_map/jit(_where)/select_n | solution.py:313
  (1 shorter events, 0.0 us)
Async XLA Ops:
  0.7 1.4 copy-start
  2.1 1.2 copy-start.1
